TPU v7x, 32 devices: a whole 2x2x4 slice. The times are simulated.
32 devices in a mesh: seq: 16 (over z, x, core), head: 2 (over y).
Axes of the slice: x: 2, y: 2, z: 4, core: 2. Of those that a mesh axis runs over, the one named last changes fastest.
Arguments:
- queries: bfloat16 [6144, 32, 128], P(('seq', 'head')), may hold values from -6 to 6
- keys: bfloat16 [6144, 8, 128], P('seq', 'head'), may hold values from -6 to 6
- values: bfloat16 [6144, 8, 128], P('seq', 'head'), may hold values from -1.5 to 1.5
- outputs: bfloat16 [6144, 32, 128], P(('seq', 'head')), may hold values from -1.5 to 1.5
- output_gradient: bfloat16 [6144, 32, 128], P(('seq', 'head')), may hold values from -24 to 24
- lse: float32 [6144, 32], P(('seq', 'head')), may hold values from 5.5 to 7.5
Outputs:
- query_grad: bfloat16 [6144, 32, 128], P(('seq', 'head'))
- key_gradient: bfloat16 [6144, 8, 128], P('seq', 'head')
- value_gradient: bfloat16 [6144, 8, 128], P('seq', 'head')
All inputs are finite; a program needn't handle non-finite values.
Results may differ from a plain program's by a relative error of at most 0.0068.
Values may be sent and summed in bfloat16 or wider, within the bound.
No kernel may reach another device: no remote copies, remote signals or barrier semaphores. Data moves between devices by JAX's collectives and lax.ppermute only.
A program may use at most 64 MiB of HBM per device.

v0:
```python
import jax
import jax.numpy as jnp
from jax import lax
from jax.sharding import PartitionSpec as P


def shifted(shard, axis, by):
    size = lax.axis_size(axis)
    pairs = [(i, i + by) for i in range(size) if 0 <= i + by < size]
    return lax.ppermute(shard, axis, pairs)


def body(queries, keys, values, outputs, output_gradient, lse):
    row_delta = jnp.sum(output_gradient.astype(jnp.float32) * outputs.astype(jnp.float32), axis=-1)
    query_blk, grad_blk = (
        lax.all_to_all(queries, "head", split_axis=1, concat_axis=0, tiled=True),
        lax.all_to_all(output_gradient, "head", split_axis=1, concat_axis=0, tiled=True),
    )
    lse_blk, delta_blk = (
        lax.all_to_all(lse, "head", split_axis=1, concat_axis=0, tiled=True),
        lax.all_to_all(row_delta, "head", split_axis=1, concat_axis=0, tiled=True),
    )
    token_length = keys.shape[0]
    heads_kv = keys.shape[1]
    head_dim = keys.shape[2]
    heads_query = query_blk.shape[1]
    query_groups = heads_query // heads_kv
    score_scale = head_dim ** (-0.5)
    near_key, near_value = shifted((keys, values), "seq", 1)
    far_key, far_value = shifted((keys, values), "seq", 2)
    key_cat = jnp.concatenate([far_key, near_key, keys], 0)
    value_cat = jnp.concatenate([far_value, near_value, values], 0)
    block_start = lax.axis_index("seq") * token_length
    row_ids = jnp.arange(token_length, dtype=jnp.int32)[:, None]
    col_ids = jnp.arange(3 * token_length, dtype=jnp.int32)[None, :]
    allowed = (
        (block_start - 2 * token_length + col_ids >= 0)
        & (col_ids > row_ids)
        & (col_ids <= row_ids + 2 * token_length)
    )
    query_four = query_blk.reshape(token_length, heads_kv, query_groups, head_dim)
    grad_four = grad_blk.reshape(token_length, heads_kv, query_groups, head_dim)
    lse_three = lse_blk.reshape(token_length, heads_kv, query_groups)
    delta_three = delta_blk.reshape(token_length, heads_kv, query_groups)
    query_list = []
    key_list = []
    value_list = []
    for group in range(heads_kv):
        query_one = query_four[:, group]
        grad_one = grad_four[:, group]
        lse_one = lse_three[:, group]
        delta_one = delta_three[:, group]
        key_one = key_cat[:, group]
        value_one = value_cat[:, group]
        scores = (
            jnp.einsum("tgd,cd->tgc", query_one, key_one, preferred_element_type=jnp.float32)
            * score_scale
        )
        attn_prob = jnp.where(allowed[:, None, :], jnp.exp(scores - lse_one[..., None]), 0.0)
        prob_bf = attn_prob.astype(jnp.bfloat16)
        val_part = jnp.einsum("tgc,tgd->cd", prob_bf, grad_one, preferred_element_type=jnp.float32)
        prob_grad = jnp.einsum(
            "tgd,cd->tgc", grad_one, value_one, preferred_element_type=jnp.float32
        )
        score_bf = (attn_prob * (prob_grad - delta_one[..., None]) * score_scale).astype(
            jnp.bfloat16
        )
        query_part = jnp.einsum(
            "tgc,cd->tgd", score_bf, key_one, preferred_element_type=jnp.float32
        ).astype(jnp.bfloat16)
        key_part = jnp.einsum(
            "tgc,tgd->cd", score_bf, query_one, preferred_element_type=jnp.float32
        )
        query_list.append(query_part)
        key_list.append(key_part)
        value_list.append(val_part)
    query_local = jnp.stack(query_list, 1).reshape(token_length, heads_query, head_dim)
    key_all = jnp.stack(key_list, 1)
    value_all = jnp.stack(value_list, 1)
    own_key = key_all[2 * token_length :]
    own_value = value_all[2 * token_length :]
    prev_key = key_all[token_length : 2 * token_length]
    prev_value = value_all[token_length : 2 * token_length]
    back_key = key_all[:token_length]
    back_value = value_all[:token_length]
    held_key, held_value = shifted((back_key, back_value), "seq", -1)
    came_key, came_value = shifted((prev_key + held_key, prev_value + held_value), "seq", -1)
    key_total = own_key + came_key
    value_total = own_value + came_value
    query_grad = lax.all_to_all(query_local, "head", split_axis=0, concat_axis=1, tiled=True)
    return (query_grad, key_total.astype(jnp.bfloat16), value_total.astype(jnp.bfloat16))


def solution(mesh):
    return jax.shard_map(
        body,
        mesh=mesh,
        in_specs=(
            P(("seq", "head"), None, None),
            P("seq", "head", None),
            P("seq", "head", None),
            P(("seq", "head"), None, None),
            P(("seq", "head"), None, None),
            P(("seq", "head"), None),
        ),
        out_specs=(P(("seq", "head"), None, None), P("seq", "head", None), P("seq", "head", None)),
        check_vma=False,
    )
```

profile of v0, /device:TPU:16, one launch (start us, length us, event | category | flops | bytes accessed | tf_op | source)
XLA Modules:
  0.0 141.0 jit_solution(12212397745804312269)
XLA Ops:
  0.6 1.9 %copy.64 = bf16[384,4,128]{2,0,1:T(8,128)(2,1)} copy(bf16[384,4,128]{2,1,0:T(4,128)(2,1)} %param.8) | data formatting | bytes 786432 | tf_op args[2]
  2.6 1.9 %collective-permute-start.3 = (bf16[384,4,128]{2,0,1:T(8,128)(2,1)}, bf16[384,4,128]{2,0,1:T(8,128)(2,1)}, u32[]{:S(2)}, u32[]{:S(2)}) collective-permute-start(bf16[384,4,128]{2,0,1:T(8,128)(2,1)} %copy.64), channel_id=1, source_target_pairs={{0,2},{2,4},{4,6},{6,8},{8,10},{10,12},{12,14},{14,16},{16,18},{18... | collective-permute-start | bytes 1179656 | tf_op jit(solution)/shard_map/ppermute | solution.py:10
  4.5 3.4 %collective-permute-start.2 = (bf16[384,4,128]{2,0,1:T(8,128)(2,1)}, bf16[384,4,128]{2,0,1:T(8,128)(2,1)}, u32[]{:S(2)}, u32[]{:S(2)}) collective-permute-start(bf16[384,4,128]{2,0,1:T(8,128)(2,1)} %copy.64), channel_id=1, source_target_pairs={{0,4},{2,6},{4,8},{6,10},{8,12},{10,14},{12,16},{14,18},{16,20},{1... | collective-permute-start | bytes 1179656 | tf_op jit(solution)/shard_map/ppermute | solution.py:10
  7.9 1.8 %copy.58 = bf16[384,4,128]{2,0,1:T(8,128)(2,1)} copy(bf16[384,4,128]{2,1,0:T(4,128)(2,1)} %param.7) | data formatting | bytes 786432 | tf_op args[1]
  9.7 3.3 %collective-permute-start.1 = (bf16[384,4,128]{2,0,1:T(8,128)(2,1)}, bf16[384,4,128]{2,0,1:T(8,128)(2,1)}, u32[]{:S(2)}, u32[]{:S(2)}) collective-permute-start(bf16[384,4,128]{2,0,1:T(8,128)(2,1)} %copy.58), channel_id=1, source_target_pairs={{0,2},{2,4},{4,6},{6,8},{8,10},{10,12},{12,14},{14,16},{16,18},{18... | collective-permute-start | bytes 1179656 | tf_op jit(solution)/shard_map/ppermute | solution.py:10
  13.0 3.4 %collective-permute-start = (bf16[384,4,128]{2,0,1:T(8,128)(2,1)}, bf16[384,4,128]{2,0,1:T(8,128)(2,1)}, u32[]{:S(2)}, u32[]{:S(2)}) collective-permute-start(bf16[384,4,128]{2,0,1:T(8,128)(2,1)} %copy.58), channel_id=1, source_target_pairs={{0,4},{2,6},{4,8},{6,10},{8,12},{10,14},{12,16},{14,18},{16,20},{1... | collective-permute-start | bytes 1179656 | tf_op jit(solution)/shard_map/ppermute | solution.py:10
  16.4 3.3 %all-to-all-start.1 = ((f32[192,2,16]{0,2,1:T(8,128)}), f32[192,2,16]{0,2,1:T(8,128)S(1)}, u32[]{:S(2)}, u32[]{:S(2)}) async-start(f32[192,2,16]{0,2,1:T(8,128)} %bitcast.198), calls=%async_computation.1 | async-start | bytes 65536 | tf_op jit(solution)/shard_map/all_to_all | solution.py:20
  19.7 2.3 %multiply_reduce_fusion = f32[192,32]{1,0:T(8,128)S(1)} fusion(bf16[192,32,128]{2,1,0:T(8,128)(2,1)} %param.9, bf16[192,32,128]{2,1,0:T(8,128)(2,1)S(1)} %copy-done.1), kind=kLoop, calls=%fused_computation.24 | loop fusion | flops 3139584 | bytes 3170304 | tf_op jit(solution)/shard_map/reduce_sum | solution.py:14
  23.6 3.3 %all-to-all-start.3 = ((f32[192,2,16]{0,2,1:T(8,128)}), f32[192,2,16]{0,2,1:T(8,128)S(1)}, u32[]{:S(2)}, u32[]{:S(2)}) async-start(f32[192,2,16]{0,2,1:T(8,128)} %bitcast.16), calls=%async_computation.3 | async-start | bytes 65536 | tf_op jit(solution)/shard_map/all_to_all | solution.py:21
  26.9 1.8 %copy.61 = bf16[192,32,128]{2,0,1:T(8,128)(2,1)} copy(bf16[192,32,128]{2,1,0:T(8,128)(2,1)S(1)} %copy-done.4) | data formatting | bytes 3145728 | tf_op args[0]
  28.7 2.2 %all-to-all-done.3 = f32[192,2,16]{0,2,1:T(8,128)S(1)} async-done(((f32[192,2,16]{0,2,1:T(8,128)}), f32[192,2,16]{0,2,1:T(8,128)S(1)}, u32[]{:S(2)}, u32[]{:S(2)}) %all-to-all-start.3) | async-done | bytes 24608 | tf_op jit(solution)/shard_map/all_to_all | solution.py:21
  30.8 3.7 %all-to-all-start = ((bf16[192,32,128]{2,0,1:T(8,128)(2,1)}), bf16[192,32,128]{2,0,1:T(8,128)(2,1)S(1)}, u32[]{:S(2)}, u32[]{:S(2)}) async-start(bf16[192,32,128]{2,0,1:T(8,128)(2,1)} %copy.61), calls=%async_computation | async-start | bytes 3145728 | tf_op jit(solution)/shard_map/all_to_all | solution.py:16
  34.5 1.2 fusion.29
  35.7 1.8 %copy.67 = bf16[192,32,128]{2,0,1:T(8,128)(2,1)} copy(bf16[192,32,128]{2,1,0:T(8,128)(2,1)S(1)} %copy-done.1) | data formatting | bytes 3145728 | tf_op args[4]
  37.7 1.8 %constant_dynamic-update-slice_fusion.2 = bf16[1152,4,128]{2,0,1:T(8,128)(2,1)} fusion(bf16[384,4,128]{2,0,1:T(8,128)(2,1)} %collective-permute-done), kind=kLoop, calls=%fused_computation.72 | loop fusion | bytes 786432
  39.5 13.1 %all-to-all-done = bf16[192,32,128]{2,0,1:T(8,128)(2,1)S(1)} async-done(((bf16[192,32,128]{2,0,1:T(8,128)(2,1)}), bf16[192,32,128]{2,0,1:T(8,128)(2,1)S(1)}, u32[]{:S(2)}, u32[]{:S(2)}) %all-to-all-start) | async-done | bytes 1572896 | tf_op jit(solution)/shard_map/all_to_all | solution.py:16
  52.6 4.8 %all-to-all-start.2 = ((bf16[192,32,128]{2,0,1:T(8,128)(2,1)}), bf16[192,32,128]{2,0,1:T(8,128)(2,1)}, u32[]{:S(2)}, u32[]{:S(2)}) async-start(bf16[192,32,128]{2,0,1:T(8,128)(2,1)} %copy.67), calls=%async_computation.2 | async-start | bytes 3145728 | tf_op jit(solution)/shard_map/all_to_all | solution.py:17
  58.6 1.8 %constant_dynamic-update-slice_fusion.1 = bf16[1152,4,128]{2,0,1:T(8,128)(2,1)} fusion(bf16[1152,4,128]{2,0,1:T(8,128)(2,1)} %constant_dynamic-update-slice_fusion.2, bf16[384,4,128]{2,0,1:T(8,128)(2,1)} %collective-permute-done.1), kind=kLoop, calls=%fused_computation.71 | loop fusion | bytes 786432
  63.5 11.1 %all-to-all-done.2 = bf16[192,32,128]{2,0,1:T(8,128)(2,1)} async-done(((bf16[192,32,128]{2,0,1:T(8,128)(2,1)}), bf16[192,32,128]{2,0,1:T(8,128)(2,1)}, u32[]{:S(2)}, u32[]{:S(2)}) %all-to-all-start.2) | async-done | bytes 1572896 | tf_op jit(solution)/shard_map/all_to_all | solution.py:17
  74.7 1.5 %copy.68 = bf16[192,2,16,128]{3,0,1,2:T(8,128)(2,1)S(1)} copy(bf16[192,2,16,128]{3,0,2,1:T(8,128)(2,1)} %bitcast.12) | data formatting | bytes 3145728 | tf_op jit(solution)/shard_map/all_to_all | solution.py:17
  76.2 1.8 %bitcast_select_fusion = f32[384,4,1152]{0,2,1:T(8,128)S(1)} fusion(f32[384,4]{0,1:T(4,128)S(1)} %get-tuple-element.20, pred[384,1152]{0,1:T(8,128)(4,1)S(1)} %copy-done.7, bf16[384,4,4,128]{3,0,2,1:T(8,128)(2,1)S(1)} %bitcast.186, bf16[1152,4,128]{2,0,1:T(8,128)(2,1)S(1)} %copy-done.8), kind=kOutput, calls=%fused_computation.3 | convolution fusion | flops 458293248 | bytes 8214528 | tf_op jit(solution)/shard_map/tgd,cd->tgc/dot_general | solution.py:56
  79.3 1.1 fusion.1
  80.4 1.2 fusion.33
  81.6 1.1 convolution_bitcast_fusion
  82.7 1.8 %bitcast_select_fusion.1 = f32[384,4,1152]{0,2,1:T(8,128)S(1)} fusion(f32[384,4]{0,1:T(4,128)S(1)} %get-tuple-element.21, pred[384,1152]{0,1:T(8,128)(4,1)S(1)} %copy-done.7, bf16[384,4,4,128]{3,0,2,1:T(8,128)(2,1)S(1)} %bitcast.188, bf16[1152,4,128]{2,0,1:T(8,128)(2,1)S(1)} %copy-done.8), kind=kOutput, calls=%fused_computation.7 | convolution fusion | flops 458293248 | bytes 8214528 | tf_op jit(solution)/shard_map/tgd,cd->tgc/dot_general | solution.py:56
  85.6 1.1 fusion.3
  86.7 1.2 fusion.32
  87.9 1.1 convolution_bitcast_fusion.1
  89.0 2.0 %bitcast_select_fusion.2 = f32[384,4,1152]{0,2,1:T(8,128)S(1)} fusion(f32[384,4]{0,1:T(4,128)S(1)} %get-tuple-element.22, pred[384,1152]{0,1:T(8,128)(4,1)S(1)} %copy-done.7, bf16[384,4,4,128]{3,0,2,1:T(8,128)(2,1)S(1)} %bitcast.190, bf16[1152,4,128]{2,0,1:T(8,128)(2,1)S(1)} %copy-done.8), kind=kOutput, calls=%fused_computation.11 | convolution fusion | flops 458293248 | bytes 8214528 | tf_op jit(solution)/shard_map/tgd,cd->tgc/dot_general | solution.py:56
  92.1 1.1 fusion.5
  93.3 1.1 convolution_bitcast_fusion.2
  94.4 1.8 %bitcast_select_fusion.3 = f32[384,4,1152]{0,2,1:T(8,128)S(1)} fusion(f32[384,4]{0,1:T(4,128)S(1)} %get-tuple-element.19, pred[384,1152]{0,1:T(8,128)(4,1)S(1)} %copy-done.7, bf16[384,4,4,128]{3,0,2,1:T(8,128)(2,1)S(1)} %bitcast.192, bf16[1152,4,128]{2,0,1:T(8,128)(2,1)S(1)} %copy-done.8), kind=kOutput, calls=%fused_computation.15 | convolution fusion | flops 458293248 | bytes 8214528 | tf_op jit(solution)/shard_map/tgd,cd->tgc/dot_general | solution.py:56
  97.3 1.1 fusion.7
  98.4 1.1 convolution_bitcast_fusion.3
  100.8 1.9 %collective-permute-start.4 = (f32[384,4,128]{2,0,1:T(8,128)}, f32[384,4,128]{2,0,1:T(8,128)}, u32[]{:S(2)}, u32[]{:S(2)}) collective-permute-start(f32[384,4,128]{2,0,1:T(8,128)} %slice.146), channel_id=1, source_target_pairs={{2,0},{4,2},{6,4},{8,6},{10,8},{12,10},{14,12},{16,14},{18,16},{20... | collective-permute-start | bytes 2359304 | tf_op jit(solution)/shard_map/ppermute | solution.py:10
  102.8 2.9 %collective-permute-start.6 = (f32[384,4,128]{2,0,1:T(8,128)S(1)}, f32[384,4,128]{2,0,1:T(8,128)}, u32[]{:S(2)}, u32[]{:S(2)}) collective-permute-start(f32[384,4,128]{2,0,1:T(8,128)S(1)} %slice.149), channel_id=1, source_target_pairs={{2,0},{4,2},{6,4},{8,6},{10,8},{12,10},{14,12},{16,14},{18,16},{20... | collective-permute-start | bytes 2359304 | tf_op jit(solution)/shard_map/ppermute | solution.py:10
  105.7 1.2 fusion.31
  106.8 1.2 fusion.30
  108.2 2.2 %copy.75 = bf16[384,16,128]{2,1,0:T(8,128)(2,1)} copy(bf16[384,16,128]{2,0,1:T(8,128)(2,1)S(1)} %bitcast.194) | data formatting | bytes 3145728 | tf_op jit(solution)/shard_map/reshape | solution.py:77
  110.4 4.6 %all-to-all-start.4 = ((bf16[384,16,128]{2,1,0:T(8,128)(2,1)}), bf16[384,16,128]{2,1,0:T(8,128)(2,1)}, u32[]{:S(2)}, u32[]{:S(2)}) async-start(bf16[384,16,128]{2,1,0:T(8,128)(2,1)} %copy.75), calls=%async_computation.4 | async-start | bytes 3145728 | tf_op jit(solution)/shard_map/all_to_all | solution.py:90
  115.0 2.3 %slice_add_fusion.2 = f32[384,4,128]{2,0,1:T(8,128)} fusion(f32[384,4,128]{2,0,1:T(8,128)} %collective-permute-done.4, f32[1152,4,128]{2,0,1:T(8,128)} %copy-done), kind=kLoop, calls=%fused_computation.51 | loop fusion | flops 196608 | bytes 2359296 | tf_op jit(solution)/shard_map/add | solution.py:87
  117.3 2.3 %collective-permute-start.5 = (f32[384,4,128]{2,0,1:T(8,128)}, f32[384,4,128]{2,0,1:T(8,128)}, u32[]{:S(2)}, u32[]{:S(2)}) collective-permute-start(f32[384,4,128]{2,0,1:T(8,128)} %slice_add_fusion.2), channel_id=1, source_target_pairs={{2,0},{4,2},{6,4},{8,6},{10,8},{12,10},{14,12},{16,14},{18,16},{20... | collective-permute-start | bytes 2359304 | tf_op jit(solution)/shard_map/ppermute | solution.py:10
  119.6 1.3 collective-permute-done.6
  120.9 2.1 %slice_add_fusion = f32[384,4,128]{2,0,1:T(8,128)} fusion(f32[384,4,128]{2,0,1:T(8,128)} %collective-permute-done.6, f32[1152,4,128]{2,0,1:T(8,128)S(1)} %pad_maximum_fusion.1), kind=kLoop, calls=%fused_computation.48 | loop fusion | flops 196608 | bytes 2359296 | tf_op jit(solution)/shard_map/add | solution.py:87
  123.0 4.8 %collective-permute-start.7 = (f32[384,4,128]{2,0,1:T(8,128)}, f32[384,4,128]{2,0,1:T(8,128)S(1)}, u32[]{:S(2)}, u32[]{:S(2)}) collective-permute-start(f32[384,4,128]{2,0,1:T(8,128)} %slice_add_fusion), channel_id=1, source_target_pairs={{2,0},{4,2},{6,4},{8,6},{10,8},{12,10},{14,12},{16,14},{18,16},{20... | collective-permute-start | bytes 2359304 | tf_op jit(solution)/shard_map/ppermute | solution.py:10
  127.8 6.7 %all-to-all-done.4 = bf16[384,16,128]{2,1,0:T(8,128)(2,1)} async-done(((bf16[384,16,128]{2,1,0:T(8,128)(2,1)}), bf16[384,16,128]{2,1,0:T(8,128)(2,1)}, u32[]{:S(2)}, u32[]{:S(2)}) %all-to-all-start.4) | async-done | bytes 1572896 | tf_op jit(solution)/shard_map/all_to_all | solution.py:90
  134.5 2.8 %copy.76 = bf16[192,2,16,128]{3,2,1,0:T(8,128)(2,1)} copy(bf16[192,2,16,128]{3,2,0,1:T(8,128)(2,1)} %bitcast.58) | data formatting | bytes 3145728 | tf_op jit(solution)/shard_map/all_to_all | solution.py:90
  137.4 1.5 %fusion.35 = bf16[384,4,128]{2,0,1:T(8,128)(2,1)S(1)} fusion(f32[384,4,128]{2,0,1:T(8,128)} %collective-permute-done.5, f32[1152,4,128]{2,0,1:T(8,128)} %copy-done), kind=kLoop, calls=%fused_computation.53 | loop fusion | flops 393216 | bytes 1966080 | tf_op jit(solution)/shard_map/convert_element_type | solution.py:91
  (54 shorter events, 14.3 us)
Async XLA Ops:
  0.6 19.1 %copy-start.1 = (bf16[192,32,128]{2,1,0:T(8,128)(2,1)S(1)}, bf16[192,32,128]{2,1,0:T(8,128)(2,1)}, u32[]{:S(2)}) copy-start(bf16[192,32,128]{2,1,0:T(8,128)(2,1)} %param.10) | copy-start | bytes 4718596
  0.6 26.3 %copy-start.4 = (bf16[192,32,128]{2,1,0:T(8,128)(2,1)S(1)}, bf16[192,32,128]{2,1,0:T(8,128)(2,1)}, u32[]{:S(2)}) copy-start(bf16[192,32,128]{2,1,0:T(8,128)(2,1)} %param.6) | copy-start | bytes 4718596
  2.6 57.8 %collective-permute-start.3 = (bf16[384,4,128]{2,0,1:T(8,128)(2,1)}, bf16[384,4,128]{2,0,1:T(8,128)(2,1)}, u32[]{:S(2)}, u32[]{:S(2)}) collective-permute-start(bf16[384,4,128]{2,0,1:T(8,128)(2,1)} %copy.64), channel_id=1, source_target_pairs={{0,2},{2,4},{4,6},{6,8},{8,10},{10,12},{12,14},{14,16},{16,18},{18... | collective-permute-start | bytes 1179656 | tf_op jit(solution)/shard_map/ppermute | solution.py:10
  4.5 52.9 %collective-permute-start.2 = (bf16[384,4,128]{2,0,1:T(8,128)(2,1)}, bf16[384,4,128]{2,0,1:T(8,128)(2,1)}, u32[]{:S(2)}, u32[]{:S(2)}) collective-permute-start(bf16[384,4,128]{2,0,1:T(8,128)(2,1)} %copy.64), channel_id=1, source_target_pairs={{0,4},{2,6},{4,8},{6,10},{8,12},{10,14},{12,16},{14,18},{16,20},{1... | collective-permute-start | bytes 1179656 | tf_op jit(solution)/shard_map/ppermute | solution.py:10
  9.7 48.8 %collective-permute-start.1 = (bf16[384,4,128]{2,0,1:T(8,128)(2,1)}, bf16[384,4,128]{2,0,1:T(8,128)(2,1)}, u32[]{:S(2)}, u32[]{:S(2)}) collective-permute-start(bf16[384,4,128]{2,0,1:T(8,128)(2,1)} %copy.58), channel_id=1, source_target_pairs={{0,2},{2,4},{4,6},{6,8},{8,10},{10,12},{12,14},{14,16},{16,18},{18... | collective-permute-start | bytes 1179656 | tf_op jit(solution)/shard_map/ppermute | solution.py:10
  13.0 24.7 %collective-permute-start = (bf16[384,4,128]{2,0,1:T(8,128)(2,1)}, bf16[384,4,128]{2,0,1:T(8,128)(2,1)}, u32[]{:S(2)}, u32[]{:S(2)}) collective-permute-start(bf16[384,4,128]{2,0,1:T(8,128)(2,1)} %copy.58), channel_id=1, source_target_pairs={{0,4},{2,6},{4,8},{6,10},{8,12},{10,14},{12,16},{14,18},{16,20},{1... | collective-permute-start | bytes 1179656 | tf_op jit(solution)/shard_map/ppermute | solution.py:10
  16.4 7.2 %all-to-all-start.1 = ((f32[192,2,16]{0,2,1:T(8,128)}), f32[192,2,16]{0,2,1:T(8,128)S(1)}, u32[]{:S(2)}, u32[]{:S(2)}) async-start(f32[192,2,16]{0,2,1:T(8,128)} %bitcast.198), calls=%async_computation.1 | async-start | bytes 65536 | tf_op jit(solution)/shard_map/all_to_all | solution.py:20
  23.6 7.2 %all-to-all-start.3 = ((f32[192,2,16]{0,2,1:T(8,128)}), f32[192,2,16]{0,2,1:T(8,128)S(1)}, u32[]{:S(2)}, u32[]{:S(2)}) async-start(f32[192,2,16]{0,2,1:T(8,128)} %bitcast.16), calls=%async_computation.3 | async-start | bytes 65536 | tf_op jit(solution)/shard_map/all_to_all | solution.py:21
  30.8 21.8 %all-to-all-start = ((bf16[192,32,128]{2,0,1:T(8,128)(2,1)}), bf16[192,32,128]{2,0,1:T(8,128)(2,1)S(1)}, u32[]{:S(2)}, u32[]{:S(2)}) async-start(bf16[192,32,128]{2,0,1:T(8,128)(2,1)} %copy.61), calls=%async_computation | async-start | bytes 3145728 | tf_op jit(solution)/shard_map/all_to_all | solution.py:16
  39.5 21.9 %copy-start.5 = (bf16[384,4,128]{2,1,0:T(4,128)(2,1)S(1)}, bf16[384,4,128]{2,1,0:T(4,128)(2,1)}, u32[]{:S(2)}) copy-start(bf16[384,4,128]{2,1,0:T(4,128)(2,1)} %param.7) | copy-start | bytes 1179652
  52.6 22.0 %all-to-all-start.2 = ((bf16[192,32,128]{2,0,1:T(8,128)(2,1)}), bf16[192,32,128]{2,0,1:T(8,128)(2,1)}, u32[]{:S(2)}, u32[]{:S(2)}) async-start(bf16[192,32,128]{2,0,1:T(8,128)(2,1)} %copy.67), calls=%async_computation.2 | async-start | bytes 3145728 | tf_op jit(solution)/shard_map/all_to_all | solution.py:17
  57.4 4.8 %copy-start.6 = (bf16[384,4,128]{2,1,0:T(4,128)(2,1)S(1)}, bf16[384,4,128]{2,1,0:T(4,128)(2,1)}, u32[]{:S(2)}) copy-start(bf16[384,4,128]{2,1,0:T(4,128)(2,1)} %param.8) | copy-start | bytes 1179652
  62.4 1.0 copy-start.2
  63.5 12.7 %copy-start.7 = (pred[384,1152]{0,1:T(8,128)(4,1)S(1)}, pred[384,1152]{0,1:T(8,128)(4,1)}, u32[]{:S(2)}) copy-start(pred[384,1152]{0,1:T(8,128)(4,1)} %fusion.29) | copy-start | bytes 1327108
  63.5 12.7 %copy-start.8 = (bf16[1152,4,128]{2,0,1:T(8,128)(2,1)S(1)}, bf16[1152,4,128]{2,0,1:T(8,128)(2,1)}, u32[]{:S(2)}) copy-start(bf16[1152,4,128]{2,0,1:T(8,128)(2,1)} %constant_dynamic-update-slice_fusion) | copy-start | bytes 3538948
  78.0 1.3 copy-start.3
  99.7 5.9 %copy-start.9 = (bf16[1152,4,128]{2,0,1:T(8,128)(2,1)S(1)}, bf16[1152,4,128]{2,0,1:T(8,128)(2,1)}, u32[]{:S(2)}) copy-start(bf16[1152,4,128]{2,0,1:T(8,128)(2,1)} %constant_dynamic-update-slice_fusion) | copy-start | bytes 3538948
  99.9 6.9 %copy-start = (f32[1152,4,128]{2,0,1:T(8,128)}, f32[1152,4,128]{2,0,1:T(8,128)S(1)}, u32[]{:S(2)}) copy-start(f32[1152,4,128]{2,0,1:T(8,128)S(1)} %pad_maximum_fusion) | copy-start | bytes 7077892
  100.8 14.2 %collective-permute-start.4 = (f32[384,4,128]{2,0,1:T(8,128)}, f32[384,4,128]{2,0,1:T(8,128)}, u32[]{:S(2)}, u32[]{:S(2)}) collective-permute-start(f32[384,4,128]{2,0,1:T(8,128)} %slice.146), channel_id=1, source_target_pairs={{2,0},{4,2},{6,4},{8,6},{10,8},{12,10},{14,12},{16,14},{18,16},{20... | collective-permute-start | bytes 2359304 | tf_op jit(solution)/shard_map/ppermute | solution.py:10
  102.8 18.1 %collective-permute-start.6 = (f32[384,4,128]{2,0,1:T(8,128)S(1)}, f32[384,4,128]{2,0,1:T(8,128)}, u32[]{:S(2)}, u32[]{:S(2)}) collective-permute-start(f32[384,4,128]{2,0,1:T(8,128)S(1)} %slice.149), channel_id=1, source_target_pairs={{2,0},{4,2},{6,4},{8,6},{10,8},{12,10},{14,12},{16,14},{18,16},{20... | collective-permute-start | bytes 2359304 | tf_op jit(solution)/shard_map/ppermute | solution.py:10
  110.4 24.2 %all-to-all-start.4 = ((bf16[384,16,128]{2,1,0:T(8,128)(2,1)}), bf16[384,16,128]{2,1,0:T(8,128)(2,1)}, u32[]{:S(2)}, u32[]{:S(2)}) async-start(bf16[384,16,128]{2,1,0:T(8,128)(2,1)} %copy.75), calls=%async_computation.4 | async-start | bytes 3145728 | tf_op jit(solution)/shard_map/all_to_all | solution.py:90
  117.3 20.0 %collective-permute-start.5 = (f32[384,4,128]{2,0,1:T(8,128)}, f32[384,4,128]{2,0,1:T(8,128)}, u32[]{:S(2)}, u32[]{:S(2)}) collective-permute-start(f32[384,4,128]{2,0,1:T(8,128)} %slice_add_fusion.2), channel_id=1, source_target_pairs={{2,0},{4,2},{6,4},{8,6},{10,8},{12,10},{14,12},{16,14},{18,16},{20... | collective-permute-start | bytes 2359304 | tf_op jit(solution)/shard_map/ppermute | solution.py:10
  123.0 16.9 %collective-permute-start.7 = (f32[384,4,128]{2,0,1:T(8,128)}, f32[384,4,128]{2,0,1:T(8,128)S(1)}, u32[]{:S(2)}, u32[]{:S(2)}) collective-permute-start(f32[384,4,128]{2,0,1:T(8,128)} %slice_add_fusion), channel_id=1, source_target_pairs={{2,0},{4,2},{6,4},{8,6},{10,8},{12,10},{14,12},{16,14},{18,16},{20... | collective-permute-start | bytes 2359304 | tf_op jit(solution)/shard_map/ppermute | solution.py:10
where the time goes:
time: 142 us; the launch traced here: 141 us
  starting transfers between devices  43.5 us (31%)
  waiting for transfers between devices  35.4 us (25%)
  local copies, waits for them, and re-layouts  25.8 us (18%)
  matrix products  25.3 us (18%)
  other arithmetic  9.93 us (7%)
    ppermute x8, starting transfers between devices, shifted(): return lax.ppermute(shard, axis, pairs)  23.8 us
    unnamed x30, local copies, waits for them, and re-layouts  16.4 us
    all_to_all x1, waiting for transfers between devices, body(): lax.all_to_all(queries, 'head', split_axis=1, concat_axis=0, tiled=True)  13.1 us
    all_to_all x1, waiting for transfers between devices, body(): lax.all_to_all(output_gradient, 'head', split_axis=1, concat_axis=0, tile...  11.1 us
    dot_general x4, matrix products, body(): jnp.einsum('tgd,cd->tgc', query_one, key_one, preferred_element_type=jnp....  7.43 us
    all_to_all x1, waiting for transfers between devices, body(): lax.all_to_all(query_local, 'head', split_axis=0, concat_axis=1, tiled=True)  6.75 us
    all_to_all x1, starting transfers between devices, body(): lax.all_to_all(output_gradient, 'head', split_axis=1, concat_axis=0, tile...  4.8 us
    dot_general x4, matrix products, body(): jnp.einsum('tgc,cd->tgd', score_bf, key_one, preferred_element_type=jnp.f...  4.64 us
  transfers between devices with their start and end apart: 13, of which 6 were waited for; matrix products, arithmetic and copies ran while one was open for 22% of the time, Pallas kernels for 0%

commit v1 on v0

v1 whole, which is shorter than its diff:
```python
import functools
import math

import jax
import jax.numpy as jnp
from jax import lax
from jax.experimental import pallas as pl
from jax.experimental.pallas import tpu as pltpu
from jax.sharding import PartitionSpec as P

LOG2E = math.log2(math.e)
F32 = jnp.float32
BF16 = jnp.bfloat16


def shifted(shard, axis, by):
    size = lax.axis_size(axis)
    pairs = [(i, i + by) for i in range(size) if 0 <= i + by < size]
    return lax.ppermute(shard, axis, pairs)


def swapped(shard, axis):
    return lax.ppermute(shard, axis, [(0, 1), (1, 0)])


def dot(a, b, dims):
    return lax.dot_general(a, b, (dims, ((), ())), preferred_element_type=F32)


def attn_kernel(half, scale, off_ref, *refs):
    (qa, ga, la, da, qb, gb, lb, db, kf, kn, ko, vf, vn, vo) = refs[:14]
    (dqa, dqb, back, prev, own) = refs[14:19]
    (kcat, vcat, dkacc, dvacc, dqacc) = refs[19:]
    length = 2 * half
    for i, (k, v) in enumerate(((kf, vf), (kn, vn), (ko, vo))):
        kcat[pl.ds(i * length, length), :] = k[0]
        vcat[pl.ds(i * length, length), :] = v[0]
    dkacc[...] = jnp.zeros_like(dkacc)
    dvacc[...] = jnp.zeros_like(dvacc)
    rows = qa.shape[1]
    token = lax.broadcasted_iota(jnp.int32, (1, rows), 1)
    token = lax.rem(token, half)
    key_id = lax.broadcasted_iota(jnp.int32, (half, 1), 0)
    tiles = 5
    for i, (q, g, l, d, dq) in enumerate(((qa, ga, la, da, dqa), (qb, gb, lb, db, dqb))):
        off = pl.multiple_of(off_ref[i], half)
        for j in range(tiles):
            span = pl.ds(pl.multiple_of(off + j * half, half), half)
            key = kcat[span, :]
            value = vcat[span, :]
            x = dot(key, q[0], ((1,), (1,))) * (scale * LOG2E) - l[0]
            p = jnp.exp2(x)
            if j == 0:
                p = jnp.where(key_id > token, p, 0.0)
            if j == tiles - 1:
                p = jnp.where(key_id <= token, p, 0.0)
            dvacc[span, :] += dot(p.astype(BF16), g[0], ((1,), (0,)))
            dp = dot(value, g[0], ((1,), (1,)))
            ds = (p * (dp - d[0]) * scale).astype(BF16)
            dkacc[span, :] += dot(ds, q[0], ((1,), (0,)))
            dq_part = dot(ds, key, ((0,), (0,)))
            if j == 0:
                dqacc[...] = dq_part
            elif j < tiles - 1:
                dqacc[...] += dq_part
            else:
                dq[0] = (dqacc[...] + dq_part).astype(BF16)
    for i, acc in enumerate((dkacc, dvacc)):
        back[i, 0] = acc[pl.ds(0, length), :].astype(BF16)
        prev[i, 0] = acc[pl.ds(length, length), :]
        own[i, 0] = acc[pl.ds(2 * length, length), :]


def attention(offs, own_rows, far_rows, kv, first, groups, scale):
    rows, head_dim = own_rows[0].shape[1:]
    length = kv[0].shape[1]
    half = length // 2
    row_spec = pl.BlockSpec((1, rows, head_dim), lambda g, off: (g, 0, 0))
    stat_spec = pl.BlockSpec((1, 1, rows), lambda g, off: (g, 0, 0))
    kv_spec = pl.BlockSpec((1, length, head_dim), lambda g, off: (g + first, 0, 0))
    kv_out = pl.BlockSpec((2, 1, length, head_dim), lambda g, off: (0, g, 0, 0))
    flops = 2 * 2 * 5 * 5 * groups * rows * half * head_dim
    return pl.pallas_call(
        functools.partial(attn_kernel, half, scale),
        grid_spec=pltpu.PrefetchScalarGridSpec(
            num_scalar_prefetch=1,
            grid=(groups,),
            in_specs=[row_spec, row_spec, stat_spec, stat_spec] * 2 + [kv_spec] * 6,
            out_specs=[row_spec, row_spec, kv_out, kv_out, kv_out],
            scratch_shapes=[
                pltpu.VMEM((3 * length, head_dim), BF16),
                pltpu.VMEM((3 * length, head_dim), BF16),
                pltpu.VMEM((3 * length, head_dim), F32),
                pltpu.VMEM((3 * length, head_dim), F32),
                pltpu.VMEM((rows, head_dim), F32),
            ],
        ),
        out_shape=[
            jax.ShapeDtypeStruct((groups, rows, head_dim), BF16),
            jax.ShapeDtypeStruct((groups, rows, head_dim), BF16),
            jax.ShapeDtypeStruct((2, groups, length, head_dim), BF16),
            jax.ShapeDtypeStruct((2, groups, length, head_dim), F32),
            jax.ShapeDtypeStruct((2, groups, length, head_dim), F32),
        ],
        cost_estimate=pl.CostEstimate(
            flops=flops, bytes_accessed=groups * length * head_dim * 60, transcendentals=0
        ),
        name="attention_backward",
    )(offs, *own_rows, *far_rows, *kv)


def body(chunks, queries, keys, values, outputs, output_gradient, lse):
    tokens, heads_all, head_dim = queries.shape
    length, heads_kv, _ = keys.shape
    side = lax.axis_index("head")
    heads = heads_all // lax.axis_size("head")
    per_kv = heads // heads_kv
    groups = heads_kv // chunks
    heads_chunk = heads // chunks
    rows = per_kv * tokens
    scale = head_dim ** (-0.5)

    def piece(x, whose, i):
        x = lax.dynamic_slice_in_dim(x, whose * heads + i * heads_chunk, heads_chunk, 1)
        return x.transpose(1, 0, 2)

    sent = []
    for i in range(chunks):
        sent.append([swapped(piece(x, 1 - side, i), "head") for x in (queries, output_gradient)])
    keys_t = keys.transpose(1, 0, 2)
    near_key = shifted(keys_t, "seq", 1)
    values_t = values.transpose(1, 0, 2)
    near_value = shifted(values_t, "seq", 1)
    delta = jnp.sum(output_gradient.astype(F32) * outputs.astype(F32), axis=-1)
    stats = jnp.stack([(lse * LOG2E).T, delta.T]).reshape(2, -1, 1, rows)
    stats_own = lax.dynamic_slice_in_dim(stats, side * heads_kv, heads_kv, 1)
    stats_far = swapped(lax.dynamic_slice_in_dim(stats, (1 - side) * heads_kv, heads_kv, 1), "head")
    far_key, far_value = shifted((near_key, near_value), "seq", 1)
    kv = (far_key, near_key, keys_t, far_value, near_value, values_t)
    offs = jnp.stack([side, 1 - side]).astype(jnp.int32) * tokens

    own_list, got_list, dkey_list = [], [], []
    for i in range(chunks):
        pick = slice(i * groups, (i + 1) * groups)
        own_rows = [piece(x, side, i).reshape(groups, rows, head_dim) for x in (queries, output_gradient)]
        far_rows = [x.reshape(groups, rows, head_dim) for x in sent[i]]
        dqa, dqb, back, prev, own = attention(
            offs,
            (*own_rows, stats_own[0, pick], stats_own[1, pick]),
            (*far_rows, stats_far[0, pick], stats_far[1, pick]),
            kv,
            i * groups,
            groups,
            scale,
        )
        got_list.append(swapped(dqb.reshape(heads_chunk, tokens, head_dim).transpose(1, 0, 2), "head"))
        own_list.append(dqa.reshape(heads_chunk, tokens, head_dim).transpose(1, 0, 2))
        held = shifted(back, "seq", -1)
        came = shifted((prev + held.astype(F32)).astype(BF16), "seq", -1)
        dkey_list.append((own + came.astype(F32)).astype(BF16))
    query_grad = jnp.zeros(queries.shape, BF16)
    for i in range(chunks):
        query_grad = lax.dynamic_update_slice_in_dim(query_grad, own_list[i], side * heads + i * heads_chunk, 1)
    for i in range(chunks):
        query_grad = lax.dynamic_update_slice_in_dim(query_grad, got_list[i], (1 - side) * heads + i * heads_chunk, 1)
    kv_grad = jnp.concatenate(dkey_list, 1).transpose(0, 2, 1, 3)
    return query_grad, kv_grad[0], kv_grad[1]


def solution(mesh):
    assert mesh.shape["head"] == 2
    return jax.shard_map(
        functools.partial(body, 2),
        mesh=mesh,
        in_specs=(
            P(("seq", "head"), None, None),
            P("seq", "head", None),
            P("seq", "head", None),
            P(("seq", "head"), None, None),
            P(("seq", "head"), None, None),
            P(("seq", "head"), None),
        ),
        out_specs=(P(("seq", "head"), None, None), P("seq", "head", None), P("seq", "head", None)),
        check_vma=False,
    )
```

time: 142 us -> 106 us (0.75)
  Pallas kernels: 0 us -> 29.2 us
  matrix products: 25.3 us -> 0 us
  waiting for transfers between devices: 35.4 us -> 18.5 us
  starting transfers between devices: 43.5 us -> 29.4 us
  other arithmetic: 9.93 us -> 3.14 us
  local copies, waits for them, and re-layouts: 25.8 us -> 24.1 us
    all_to_all x5 -> x0, waiting for transfers between devices: 34.1 us -> none  [the longest x1 13.1 us: body(): lax.all_to_all(queries, 'head', split_axis=1, concat_axis=0, tiled=True)]
    pallas_call x0 -> x2, Pallas kernels: none -> 29.2 us  [attention(): pl.pallas_call(functools.partial(attn_kernel, half, scale), grid_spec=plt...]
    dot_general x20 -> x0, matrix products: 25.3 us -> none  [the longest x4 7.43 us: body(): jnp.einsum('tgd,cd->tgc', query_one, key_one, preferred_element_type=jnp....]
    all_to_all x5 -> x0, starting transfers between devices: 19.6 us -> none  [the longest x1 4.8 us: body(): lax.all_to_all(output_gradient, 'head', split_axis=1, concat_axis=0, tile...]
    ppermute x0 -> x7, waiting for transfers between devices: none -> 18.5 us  [swapped(): return lax.ppermute(shard, axis, [(0, 1), (1, 0)])]
    unnamed x30 -> x45, local copies, waits for them, and re-layouts: 16.4 us -> 6.39 us
    transpose x0 -> x7, local copies, waits for them, and re-layouts: none -> 7.99 us  [the longest x6 7.03 us: piece(): return x.transpose(1, 0, 2)]
    ppermute x0 -> x7, starting transfers between devices: none -> 7.7 us  [swapped(): return lax.ppermute(shard, axis, [(0, 1), (1, 0)])]
  transfers between devices with their start and end apart: 13 -> 15, of which waited for: 6 -> 5; matrix products, arithmetic and copies ran while one was open for 22% -> 19% of each run, Pallas kernels for 0% -> 14%
where the time goes in v1:
time: 106 us; the launch traced here: 105 us
  starting transfers between devices  29.4 us (28%)
  Pallas kernels  29.2 us (28%)
  local copies, waits for them, and re-layouts  24.1 us (23%)
  waiting for transfers between devices  18.5 us (17%)
  other arithmetic  3.14 us (3%)
    pallas_call x2, Pallas kernels, attention(): pl.pallas_call(functools.partial(attn_kernel, half, scale), grid_spec=plt...  29.2 us
    ppermute x8, starting transfers between devices, shifted(): return lax.ppermute(shard, axis, pairs)  21.7 us
    ppermute x7, waiting for transfers between devices, swapped(): return lax.ppermute(shard, axis, [(0, 1), (1, 0)])  18.5 us
    ppermute x7, starting transfers between devices, swapped(): return lax.ppermute(shard, axis, [(0, 1), (1, 0)])  7.7 us
    transpose x6, local copies, waits for them, and re-layouts, piece(): return x.transpose(1, 0, 2)  7.03 us
    unnamed x45, local copies, waits for them, and re-layouts  6.39 us
    ppermute x4, local copies, waits for them, and re-layouts, swapped(): return lax.ppermute(shard, axis, [(0, 1), (1, 0)])  4.23 us
  transfers between devices with their start and end apart: 15, of which 5 were waited for; matrix products, arithmetic and copies ran while one was open for 19% of the time, Pallas kernels for 14%

profile of v1, /device:TPU:16, one launch (start us, length us, event | category | flops | bytes accessed | tf_op | source)
XLA Modules:
  0.0 105.3 jit_solution(8622761623101782989)
XLA Ops:
  0.7 2.6 %dynamic-slice_bitcast_fusion.1 = (bf16[8,192,128]{2,0,1:T(8,128)(2,1)}, bf16[8,192,128]{2,0,1:T(8,128)(2,1)}, bf16[8,192,128]{2,0,1:T(8,128)(2,1)}, bf16[8,192,128]{2,0,1:T(8,128)(2,1)S(1)}) fusion(bf16[192,32,128]{2,1,0:T(8,128)(2,1)} %param.6, s32[]{:T(128)S(6)} %select_n.31, s32[]{:T(128)S(6)} %select_n.28, s32[]{:T(128)S(6)} %select_n.12, s32[]{:T(128)S(6)} %select_n.30), kind=kLoop, calls=%fused_computation.15 | loop fusion | bytes 3145744 | tf_op jit(solution)/shard_map/transpose | solution.py:125
  3.3 1.5 %collective-permute-start = (bf16[8,192,128]{2,0,1:T(8,128)(2,1)}, bf16[8,192,128]{2,0,1:T(8,128)(2,1)}, u32[]{:S(2)}, u32[]{:S(2)}) collective-permute-start(bf16[8,192,128]{2,0,1:T(8,128)(2,1)} %get-tuple-element.34), channel_id=1, source_target_pairs={{0,1},{1,0},{2,3},{3,2},{4,5},{5,4},{6,7},{7,6},{8,9},{9,8},{10,11... | collective-permute-start | bytes 1179656 | tf_op jit(solution)/shard_map/ppermute | solution.py:23
  4.8 0.8 copy.51
  5.6 1.9 %collective-permute-start.3 = (bf16[4,384,128]{2,1,0:T(8,128)(2,1)}, bf16[4,384,128]{2,1,0:T(8,128)(2,1)}, u32[]{:S(2)}, u32[]{:S(2)}) collective-permute-start(bf16[4,384,128]{2,1,0:T(8,128)(2,1)} %bitcast.70.refs_10_), channel_id=1, source_target_pairs={{0,2},{2,4},{4,6},{6,8},{8,10},{10,12},{12,14},{14,16},{16,18},{18... | collective-permute-start | bytes 1179656 | tf_op jit(solution)/shard_map/ppermute | solution.py:19
  7.5 0.8 copy.50
  8.4 3.5 %collective-permute-start.5 = (bf16[4,384,128]{2,1,0:T(8,128)(2,1)}, bf16[4,384,128]{2,1,0:T(8,128)(2,1)}, u32[]{:S(2)}, u32[]{:S(2)}) collective-permute-start(bf16[4,384,128]{2,1,0:T(8,128)(2,1)} %bitcast.69.refs_13_), channel_id=1, source_target_pairs={{0,2},{2,4},{4,6},{6,8},{8,10},{10,12},{12,14},{14,16},{16,18},{18... | collective-permute-start | bytes 1179656 | tf_op jit(solution)/shard_map/ppermute | solution.py:19
  11.9 0.6 multiply_bitcast_fusion
  12.5 1.4 %stack.21 = f32[1,8,1,768]{3,2,1,0:T(1,128)} reshape(f32[32,192]{1,0:T(8,128)} %multiply_bitcast_fusion) | data formatting | bytes 49152 | tf_op jit(solution)/shard_map/stack | solution.py:135
  13.9 1.6 %multiply_reduce_fusion = f32[192,32]{1,0:T(8,128)} fusion(bf16[192,32,128]{2,1,0:T(8,128)(2,1)S(1)} %copy-done.1, bf16[192,32,128]{2,1,0:T(8,128)(2,1)S(1)} %copy-done), kind=kLoop, calls=%fused_computation | loop fusion | flops 3139584 | bytes 3170304 | tf_op jit(solution)/shard_map/reduce_sum | solution.py:134
  15.5 1.0 copy.27
  16.6 0.6 copy-done.13
  17.2 0.6 collective-permute-start.2
  17.8 1.2 %dynamic-slice_bitcast_fusion = (bf16[8,192,128]{2,0,1:T(8,128)(2,1)}, bf16[8,192,128]{2,0,1:T(8,128)(2,1)}, bf16[8,192,128]{2,0,1:T(8,128)(2,1)S(1)}, bf16[8,192,128]{2,0,1:T(8,128)(2,1)S(1)}) fusion(bf16[192,32,128]{2,1,0:T(8,128)(2,1)S(1)} %copy-done, s32[]{:T(128)S(6)} %select_n.31, s32[]{:T(128)S(6)} %select_n.28, s32[]{:T(128)S(6)} %select_n.12, ...), kind=kLoop, calls=%fused_computation.14 | loop fusion | bytes 3145744 | tf_op jit(solution)/shard_map/transpose | solution.py:125
  19.0 1.5 %collective-permute-start.1 = (bf16[8,192,128]{2,0,1:T(8,128)(2,1)}, bf16[8,192,128]{2,0,1:T(8,128)(2,1)S(1)}, u32[]{:S(2)}, u32[]{:S(2)}) collective-permute-start(bf16[8,192,128]{2,0,1:T(8,128)(2,1)} %get-tuple-element.30), channel_id=1, source_target_pairs={{0,1},{1,0},{2,3},{3,2},{4,5},{5,4},{6,7},{7,6},{8,9},{9,8},{10,11... | collective-permute-start | bytes 1179656 | tf_op jit(solution)/shard_map/ppermute | solution.py:23
  20.5 0.6 collective-permute-done.2
  21.1 0.5 collective-permute-start.7
  21.7 1.4 %collective-permute-start.8 = (bf16[8,192,128]{2,0,1:T(8,128)(2,1)}, bf16[8,192,128]{2,0,1:T(8,128)(2,1)S(1)}, u32[]{:S(2)}, u32[]{:S(2)}) collective-permute-start(bf16[8,192,128]{2,0,1:T(8,128)(2,1)} %get-tuple-element.29), channel_id=1, source_target_pairs={{0,1},{1,0},{2,3},{3,2},{4,5},{5,4},{6,7},{7,6},{8,9},{9,8},{10,11... | collective-permute-start | bytes 1179656 | tf_op jit(solution)/shard_map/ppermute | solution.py:23
  23.1 1.9 %collective-permute-start.4 = (bf16[4,384,128]{2,1,0:T(8,128)(2,1)}, bf16[4,384,128]{2,1,0:T(8,128)(2,1)S(1)}, u32[]{:S(2)}, u32[]{:S(2)}) collective-permute-start(bf16[4,384,128]{2,1,0:T(8,128)(2,1)} %collective-permute-done.3.refs_9_), channel_id=1, source_target_pairs={{0,2},{2,4},{4,6},{6,8},{8,10},{10,12},{12,14},{14,16},{16,18},{18... | collective-permute-start | bytes 1179656 | tf_op jit(solution)/shard_map/ppermute | solution.py:19
  25.1 3.6 %collective-permute-start.6 = (bf16[4,384,128]{2,1,0:T(8,128)(2,1)}, bf16[4,384,128]{2,1,0:T(8,128)(2,1)}, u32[]{:S(2)}, u32[]{:S(2)}) collective-permute-start(bf16[4,384,128]{2,1,0:T(8,128)(2,1)} %collective-permute-done.5.refs_12_), channel_id=1, source_target_pairs={{0,2},{2,4},{4,6},{6,8},{8,10},{10,12},{12,14},{14,16},{16,18},{18... | collective-permute-start | bytes 1179656 | tf_op jit(solution)/shard_map/ppermute | solution.py:19
  28.6 0.6 add_multiply_fusion.off_ref
  29.2 0.8 copy.25
  30.0 0.8 copy.26
  30.9 0.8 copy.33
  31.7 0.8 copy.34
  32.5 0.6 dynamic-slice_bitcast_fusion.8
  33.1 0.6 slice_bitcast_fusion.2
  33.7 1.8 %copy.28 = bf16[8,192,128]{2,1,0:T(8,128)(2,1)} copy(bf16[8,192,128]{2,0,1:T(8,128)(2,1)} %collective-permute-done) | data formatting | bytes 786432 | tf_op jit(solution)/shard_map/ppermute | solution.py:23
  35.5 0.8 copy.29
  36.3 3.2 %collective-permute-done.7 = bf16[8,192,128]{2,0,1:T(8,128)(2,1)S(1)} collective-permute-done((bf16[8,192,128]{2,0,1:T(8,128)(2,1)}, bf16[8,192,128]{2,0,1:T(8,128)(2,1)S(1)}, u32[]{:S(2)}, u32[]{:S(2)}) %collective-permute-start.7) | collective-permute-done | bytes 393248 | tf_op jit(solution)/shard_map/ppermute | solution.py:23
  39.6 0.8 copy.35
  40.4 6.4 %collective-permute-done.8 = bf16[8,192,128]{2,0,1:T(8,128)(2,1)S(1)} collective-permute-done((bf16[8,192,128]{2,0,1:T(8,128)(2,1)}, bf16[8,192,128]{2,0,1:T(8,128)(2,1)S(1)}, u32[]{:S(2)}, u32[]{:S(2)}) %collective-permute-start.8) | collective-permute-done | bytes 393248 | tf_op jit(solution)/shard_map/ppermute | solution.py:23
  46.8 0.8 copy.36
  47.6 0.7 copy-done.19
  48.3 14.5 %attention_backward.2 = (bf16[2,768,128]{2,1,0:T(8,128)(2,1)}, bf16[2,768,128]{2,1,0:T(8,128)(2,1)}, bf16[2,2,384,128]{3,2,1,0:T(8,128)(2,1)}, f32[2,2,384,128]{3,2,1,0:T(8,128)}, f32[2,2,384,128]{3,2,1,0:T(8,128)}) custom-call(s32[2]{0:T(128)} %add_multiply_fusion.off_ref, bf16[2,768,128]{2,1,0:T(8,128)(2,1)} %bitcast.74, bf16[2,768,128]{2,1,0:T(8,128)(2,1)} %bitcast.75, ...), custom_call_target="tpu_custom_call" | custom-call | flops 3774873600 | bytes 5898240 | tf_op jit(solution)/shard_map/attention_backward/pallas_call | solution.py:83
  62.8 2.1 %collective-permute-start.11 = (bf16[2,2,384,128]{3,2,1,0:T(8,128)(2,1)}, bf16[2,2,384,128]{3,2,1,0:T(8,128)(2,1)S(1)}, u32[]{:S(2)}, u32[]{:S(2)}) collective-permute-start(bf16[2,2,384,128]{3,2,1,0:T(8,128)(2,1)} %get-tuple-element.19), channel_id=1, source_target_pairs={{2,0},{4,2},{6,4},{8,6},{10,8},{12,10},{14,12},{16,14},{18,16},{20... | collective-permute-start | bytes 1179656 | tf_op jit(solution)/shard_map/ppermute | solution.py:19
  65.0 14.7 %attention_backward.3 = (bf16[2,768,128]{2,1,0:T(8,128)(2,1)}, bf16[2,768,128]{2,1,0:T(8,128)(2,1)}, bf16[2,2,384,128]{3,2,1,0:T(8,128)(2,1)}, f32[2,2,384,128]{3,2,1,0:T(8,128)}, f32[2,2,384,128]{3,2,1,0:T(8,128)}) custom-call(s32[2]{0:T(128)} %add_multiply_fusion.off_ref, bf16[2,768,128]{2,1,0:T(8,128)(2,1)} %bitcast.72, bf16[2,768,128]{2,1,0:T(8,128)(2,1)} %bitcast.73, ...), custom_call_target="tpu_custom_call" | custom-call | flops 3774873600 | bytes 5898240 | tf_op jit(solution)/shard_map/attention_backward/pallas_call | solution.py:83
  79.6 3.4 %collective-permute-start.13 = (bf16[2,2,384,128]{3,2,1,0:T(8,128)(2,1)}, bf16[2,2,384,128]{3,2,1,0:T(8,128)(2,1)S(1)}, u32[]{:S(2)}, u32[]{:S(2)}) collective-permute-start(bf16[2,2,384,128]{3,2,1,0:T(8,128)(2,1)} %get-tuple-element.22), channel_id=1, source_target_pairs={{2,0},{4,2},{6,4},{8,6},{10,8},{12,10},{14,12},{16,14},{18,16},{20... | collective-permute-start | bytes 1179656 | tf_op jit(solution)/shard_map/ppermute | solution.py:19
  83.4 1.6 %collective-permute-start.9 = (bf16[192,8,128]{2,1,0:T(8,128)(2,1)S(1)}, bf16[192,8,128]{2,1,0:T(8,128)(2,1)S(1)}, u32[]{:S(2)}, u32[]{:S(2)}) collective-permute-start(bf16[192,8,128]{2,1,0:T(8,128)(2,1)S(1)} %bitcast.80), channel_id=1, source_target_pairs={{0,1},{1,0},{2,3},{3,2},{4,5},{5,4},{6,7},{7,6},{8,9},{9,8},{10,11... | collective-permute-start | bytes 1179656 | tf_op jit(solution)/shard_map/ppermute | solution.py:23
  84.9 1.3 %copy.48 = bf16[8,192,128]{2,0,1:T(8,128)(2,1)S(1)} copy(bf16[8,192,128]{2,1,0:T(8,128)(2,1)} %bitcast.83) | data formatting | bytes 786432 | tf_op jit(solution)/shard_map/reshape | solution.py:156
  86.3 0.6 collective-permute-start.10
  87.4 0.3 bitcast_dynamic-update-slice_fusion
  88.0 1.9 %collective-permute-start.12 = (bf16[2,2,384,128]{3,2,1,0:T(8,128)(2,1)S(1)}, bf16[2,2,384,128]{3,2,1,0:T(8,128)(2,1)S(1)}, u32[]{:S(2)}, u32[]{:S(2)}) collective-permute-start(bf16[2,2,384,128]{3,2,1,0:T(8,128)(2,1)S(1)} %add_convert_fusion.3), channel_id=1, source_target_pairs={{2,0},{4,2},{6,4},{8,6},{10,8},{12,10},{14,12},{16,14},{18,16},{20... | collective-permute-start | bytes 1179656 | tf_op jit(solution)/shard_map/ppermute | solution.py:19
  90.1 3.4 %collective-permute-start.14 = (bf16[2,2,384,128]{3,2,1,0:T(8,128)(2,1)S(1)}, bf16[2,2,384,128]{3,2,1,0:T(8,128)(2,1)S(1)}, u32[]{:S(2)}, u32[]{:S(2)}) collective-permute-start(bf16[2,2,384,128]{3,2,1,0:T(8,128)(2,1)S(1)} %add_convert_fusion.1), channel_id=1, source_target_pairs={{2,0},{4,2},{6,4},{8,6},{10,8},{12,10},{14,12},{16,14},{18,16},{20... | collective-permute-start | bytes 1179656 | tf_op jit(solution)/shard_map/ppermute | solution.py:19
  93.5 1.9 %collective-permute-done.9 = bf16[192,8,128]{2,1,0:T(8,128)(2,1)S(1)} collective-permute-done((bf16[192,8,128]{2,1,0:T(8,128)(2,1)S(1)}, bf16[192,8,128]{2,1,0:T(8,128)(2,1)S(1)}, u32[]{:S(2)}, u32[]{:S(2)}) %collective-permute-start.9) | collective-permute-done | bytes 393248 | tf_op jit(solution)/shard_map/ppermute | solution.py:23
  95.5 6.3 %collective-permute-done.10 = bf16[192,8,128]{2,1,0:T(8,128)(2,1)S(1)} collective-permute-done((bf16[192,8,128]{2,1,0:T(8,128)(2,1)S(1)}, bf16[192,8,128]{2,1,0:T(8,128)(2,1)S(1)}, u32[]{:S(2)}, u32[]{:S(2)}) %collective-permute-start.10) | collective-permute-done | bytes 393248 | tf_op jit(solution)/shard_map/ppermute | solution.py:23
  102.2 0.9 copy-done.2
  103.2 1.1 copy.40
  104.3 1.1 copy.41
  (62 shorter events, 2.0 us)
Async XLA Ops:
  0.6 4.1 %copy-start.8 = (bf16[384,4,128]{2,1,0:T(4,128)(2,1)S(1)}, bf16[384,4,128]{2,1,0:T(4,128)(2,1)}, u32[]{:S(2)}) copy-start(bf16[384,4,128]{2,1,0:T(4,128)(2,1)} %param.7) | copy-start | bytes 1179652
  0.7 6.9 %copy-start.9 = (bf16[384,4,128]{2,1,0:T(4,128)(2,1)S(1)}, bf16[384,4,128]{2,1,0:T(4,128)(2,1)}, u32[]{:S(2)}) copy-start(bf16[384,4,128]{2,1,0:T(4,128)(2,1)} %param.8) | copy-start | bytes 1179652
  0.7 11.2 %copy-start.16 = (f32[192,32]{0,1:T(8,128)S(1)}, f32[192,32]{0,1:T(8,128)}, u32[]{:S(2)}) copy-start(f32[192,32]{0,1:T(8,128)} %param.11) | copy-start | bytes 73732
  0.7 13.3 %copy-start.1 = (bf16[192,32,128]{2,1,0:T(8,128)(2,1)S(1)}, bf16[192,32,128]{2,1,0:T(8,128)(2,1)}, u32[]{:S(2)}) copy-start(bf16[192,32,128]{2,1,0:T(8,128)(2,1)} %param.9) | copy-start | bytes 4718596
  3.3 10.7 %copy-start = (bf16[192,32,128]{2,1,0:T(8,128)(2,1)S(1)}, bf16[192,32,128]{2,1,0:T(8,128)(2,1)}, u32[]{:S(2)}) copy-start(bf16[192,32,128]{2,1,0:T(8,128)(2,1)} %param.10) | copy-start | bytes 4718596
  3.3 18.3 %collective-permute-start = (bf16[8,192,128]{2,0,1:T(8,128)(2,1)}, bf16[8,192,128]{2,0,1:T(8,128)(2,1)}, u32[]{:S(2)}, u32[]{:S(2)}) collective-permute-start(bf16[8,192,128]{2,0,1:T(8,128)(2,1)} %get-tuple-element.34), channel_id=1, source_target_pairs={{0,1},{1,0},{2,3},{3,2},{4,5},{5,4},{6,7},{7,6},{8,9},{9,8},{10,11... | collective-permute-start | bytes 1179656 | tf_op jit(solution)/shard_map/ppermute | solution.py:23
  5.6 17.5 %collective-permute-start.3 = (bf16[4,384,128]{2,1,0:T(8,128)(2,1)}, bf16[4,384,128]{2,1,0:T(8,128)(2,1)}, u32[]{:S(2)}, u32[]{:S(2)}) collective-permute-start(bf16[4,384,128]{2,1,0:T(8,128)(2,1)} %bitcast.70.refs_10_), channel_id=1, source_target_pairs={{0,2},{2,4},{4,6},{6,8},{8,10},{10,12},{12,14},{14,16},{16,18},{18... | collective-permute-start | bytes 1179656 | tf_op jit(solution)/shard_map/ppermute | solution.py:19
  8.4 16.7 %collective-permute-start.5 = (bf16[4,384,128]{2,1,0:T(8,128)(2,1)}, bf16[4,384,128]{2,1,0:T(8,128)(2,1)}, u32[]{:S(2)}, u32[]{:S(2)}) collective-permute-start(bf16[4,384,128]{2,1,0:T(8,128)(2,1)} %bitcast.69.refs_13_), channel_id=1, source_target_pairs={{0,2},{2,4},{4,6},{6,8},{8,10},{10,12},{12,14},{14,16},{16,18},{18... | collective-permute-start | bytes 1179656 | tf_op jit(solution)/shard_map/ppermute | solution.py:19
  13.9 1.6 %copy-start.15 = (f32[1,8,1,768]{3,2,1,0:T(1,128)S(1)}, f32[1,8,1,768]{3,2,1,0:T(1,128)}, u32[]{:S(2)}) copy-start(f32[1,8,1,768]{3,2,1,0:T(1,128)} %stack.21) | copy-start | bytes 73732
  16.6 0.6 copy-start.13
  17.2 12.0 %copy-start.3 = (bf16[8,192,128]{2,0,1:T(8,128)(2,1)S(1)}, bf16[8,192,128]{2,0,1:T(8,128)(2,1)}, u32[]{:S(2)}) copy-start(bf16[8,192,128]{2,0,1:T(8,128)(2,1)} %get-tuple-element.35) | copy-start | bytes 1179652
  17.2 3.9 %collective-permute-start.2 = (f32[2,4,1,768]{3,2,1,0:T(1,128)S(1)}, f32[2,4,1,768]{3,2,1,0:T(1,128)S(1)}, u32[]{:S(2)}, u32[]{:S(2)}) collective-permute-start(f32[2,4,1,768]{3,2,1,0:T(1,128)S(1)} %constant_dynamic-slice_fusion), channel_id=1, source_target_pairs={{0,1},{1,0},{2,3},{3,2},{4,5},{5,4},{6,7},{7,6},{8,9},{9,8},{10,11... | collective-permute-start | bytes 73736 | tf_op jit(solution)/shard_map/ppermute | solution.py:23
  19.0 16.6 %collective-permute-start.1 = (bf16[8,192,128]{2,0,1:T(8,128)(2,1)}, bf16[8,192,128]{2,0,1:T(8,128)(2,1)S(1)}, u32[]{:S(2)}, u32[]{:S(2)}) collective-permute-start(bf16[8,192,128]{2,0,1:T(8,128)(2,1)} %get-tuple-element.30), channel_id=1, source_target_pairs={{0,1},{1,0},{2,3},{3,2},{4,5},{5,4},{6,7},{7,6},{8,9},{9,8},{10,11... | collective-permute-start | bytes 1179656 | tf_op jit(solution)/shard_map/ppermute | solution.py:23
  21.1 0.6 copy-start.17
  21.1 18.5 %collective-permute-start.7 = (bf16[8,192,128]{2,0,1:T(8,128)(2,1)}, bf16[8,192,128]{2,0,1:T(8,128)(2,1)S(1)}, u32[]{:S(2)}, u32[]{:S(2)}) collective-permute-start(bf16[8,192,128]{2,0,1:T(8,128)(2,1)} %get-tuple-element.33), channel_id=1, source_target_pairs={{0,1},{1,0},{2,3},{3,2},{4,5},{5,4},{6,7},{7,6},{8,9},{9,8},{10,11... | collective-permute-start | bytes 1179656 | tf_op jit(solution)/shard_map/ppermute | solution.py:23
  21.7 25.1 %collective-permute-start.8 = (bf16[8,192,128]{2,0,1:T(8,128)(2,1)}, bf16[8,192,128]{2,0,1:T(8,128)(2,1)S(1)}, u32[]{:S(2)}, u32[]{:S(2)}) collective-permute-start(bf16[8,192,128]{2,0,1:T(8,128)(2,1)} %get-tuple-element.29), channel_id=1, source_target_pairs={{0,1},{1,0},{2,3},{3,2},{4,5},{5,4},{6,7},{7,6},{8,9},{9,8},{10,11... | collective-permute-start | bytes 1179656 | tf_op jit(solution)/shard_map/ppermute | solution.py:23
  23.1 24.4 %collective-permute-start.4 = (bf16[4,384,128]{2,1,0:T(8,128)(2,1)}, bf16[4,384,128]{2,1,0:T(8,128)(2,1)S(1)}, u32[]{:S(2)}, u32[]{:S(2)}) collective-permute-start(bf16[4,384,128]{2,1,0:T(8,128)(2,1)} %collective-permute-done.3.refs_9_), channel_id=1, source_target_pairs={{0,2},{2,4},{4,6},{6,8},{8,10},{10,12},{12,14},{14,16},{16,18},{18... | collective-permute-start | bytes 1179656 | tf_op jit(solution)/shard_map/ppermute | solution.py:19
  25.1 22.5 %collective-permute-start.6 = (bf16[4,384,128]{2,1,0:T(8,128)(2,1)}, bf16[4,384,128]{2,1,0:T(8,128)(2,1)}, u32[]{:S(2)}, u32[]{:S(2)}) collective-permute-start(bf16[4,384,128]{2,1,0:T(8,128)(2,1)} %collective-permute-done.5.refs_12_), channel_id=1, source_target_pairs={{0,2},{2,4},{4,6},{6,8},{8,10},{10,12},{12,14},{14,16},{16,18},{18... | collective-permute-start | bytes 1179656 | tf_op jit(solution)/shard_map/ppermute | solution.py:19
  29.2 3.3 %copy-start.14 = (f32[2,8,1,768]{3,2,1,0:T(1,128)S(1)}, f32[2,8,1,768]{3,2,1,0:T(1,128)}, u32[]{:S(2)}) copy-start(f32[2,8,1,768]{3,2,1,0:T(1,128)} %copy-done.13) | copy-start | bytes 147460
  29.2 3.9 %copy-start.18 = (f32[2,4,1,768]{3,2,1,0:T(1,128)S(1)}, f32[2,4,1,768]{3,2,1,0:T(1,128)}, u32[]{:S(2)}) copy-start(f32[2,4,1,768]{3,2,1,0:T(1,128)} %copy-done.17) | copy-start | bytes 73732
  47.6 0.7 copy-start.19
  62.8 24.9 %collective-permute-start.11 = (bf16[2,2,384,128]{3,2,1,0:T(8,128)(2,1)}, bf16[2,2,384,128]{3,2,1,0:T(8,128)(2,1)S(1)}, u32[]{:S(2)}, u32[]{:S(2)}) collective-permute-start(bf16[2,2,384,128]{3,2,1,0:T(8,128)(2,1)} %get-tuple-element.19), channel_id=1, source_target_pairs={{2,0},{4,2},{6,4},{8,6},{10,8},{12,10},{14,12},{16,14},{18,16},{20... | collective-permute-start | bytes 1179656 | tf_op jit(solution)/shard_map/ppermute | solution.py:19
  64.9 18.1 %copy-start.10 = (bf16[2,768,128]{2,1,0:T(8,128)(2,1)S(1)}, bf16[2,768,128]{2,1,0:T(8,128)(2,1)}, u32[]{:S(2)}) copy-start(bf16[2,768,128]{2,1,0:T(8,128)(2,1)} %get-tuple-element.15) | copy-start | bytes 1179652
  79.6 10.4 %collective-permute-start.13 = (bf16[2,2,384,128]{3,2,1,0:T(8,128)(2,1)}, bf16[2,2,384,128]{3,2,1,0:T(8,128)(2,1)S(1)}, u32[]{:S(2)}, u32[]{:S(2)}) collective-permute-start(bf16[2,2,384,128]{3,2,1,0:T(8,128)(2,1)} %get-tuple-element.22), channel_id=1, source_target_pairs={{2,0},{4,2},{6,4},{8,6},{10,8},{12,10},{14,12},{16,14},{18,16},{20... | collective-permute-start | bytes 1179656 | tf_op jit(solution)/shard_map/ppermute | solution.py:19
  83.1 4.0 %copy-start.11 = (bf16[2,768,128]{2,1,0:T(8,128)(2,1)S(1)}, bf16[2,768,128]{2,1,0:T(8,128)(2,1)}, u32[]{:S(2)}) copy-start(bf16[2,768,128]{2,1,0:T(8,128)(2,1)} %get-tuple-element.13) | copy-start | bytes 1179652
  83.4 12.1 %collective-permute-start.9 = (bf16[192,8,128]{2,1,0:T(8,128)(2,1)S(1)}, bf16[192,8,128]{2,1,0:T(8,128)(2,1)S(1)}, u32[]{:S(2)}, u32[]{:S(2)}) collective-permute-start(bf16[192,8,128]{2,1,0:T(8,128)(2,1)S(1)} %bitcast.80), channel_id=1, source_target_pairs={{0,1},{1,0},{2,3},{3,2},{4,5},{5,4},{6,7},{7,6},{8,9},{9,8},{10,11... | collective-permute-start | bytes 1179656 | tf_op jit(solution)/shard_map/ppermute | solution.py:23
  84.9 2.4 %copy-start.12 = (bf16[2,768,128]{2,1,0:T(8,128)(2,1)S(1)}, bf16[2,768,128]{2,1,0:T(8,128)(2,1)}, u32[]{:S(2)}) copy-start(bf16[2,768,128]{2,1,0:T(8,128)(2,1)} %get-tuple-element.14) | copy-start | bytes 1179652
  86.3 15.6 %collective-permute-start.10 = (bf16[192,8,128]{2,1,0:T(8,128)(2,1)S(1)}, bf16[192,8,128]{2,1,0:T(8,128)(2,1)S(1)}, u32[]{:S(2)}, u32[]{:S(2)}) collective-permute-start(bf16[192,8,128]{2,1,0:T(8,128)(2,1)S(1)} %bitcast.79), channel_id=1, source_target_pairs={{0,1},{1,0},{2,3},{3,2},{4,5},{5,4},{6,7},{7,6},{8,9},{9,8},{10,11... | collective-permute-start | bytes 1179656 | tf_op jit(solution)/shard_map/ppermute | solution.py:23
  86.8 1.1 %copy-start.6 = (f32[2,2,384,128]{3,2,1,0:T(8,128)S(1)}, f32[2,2,384,128]{3,2,1,0:T(8,128)}, u32[]{:S(2)}) copy-start(f32[2,2,384,128]{3,2,1,0:T(8,128)} %get-tuple-element.18) | copy-start | bytes 2359300
  87.0 2.9 %copy-start.7 = (f32[2,2,384,128]{3,2,1,0:T(8,128)S(1)}, f32[2,2,384,128]{3,2,1,0:T(8,128)}, u32[]{:S(2)}) copy-start(f32[2,2,384,128]{3,2,1,0:T(8,128)} %get-tuple-element.21) | copy-start | bytes 2359300
  88.0 13.9 %collective-permute-start.12 = (bf16[2,2,384,128]{3,2,1,0:T(8,128)(2,1)S(1)}, bf16[2,2,384,128]{3,2,1,0:T(8,128)(2,1)S(1)}, u32[]{:S(2)}, u32[]{:S(2)}) collective-permute-start(bf16[2,2,384,128]{3,2,1,0:T(8,128)(2,1)S(1)} %add_convert_fusion.3), channel_id=1, source_target_pairs={{2,0},{4,2},{6,4},{8,6},{10,8},{12,10},{14,12},{16,14},{18,16},{20... | collective-permute-start | bytes 1179656 | tf_op jit(solution)/shard_map/ppermute | solution.py:19
  90.0 12.0 %copy-start.4 = (f32[2,2,384,128]{3,2,1,0:T(8,128)S(1)}, f32[2,2,384,128]{3,2,1,0:T(8,128)}, u32[]{:S(2)}) copy-start(f32[2,2,384,128]{3,2,1,0:T(8,128)} %get-tuple-element.17) | copy-start | bytes 2359300
  90.1 12.0 %copy-start.5 = (f32[2,2,384,128]{3,2,1,0:T(8,128)S(1)}, f32[2,2,384,128]{3,2,1,0:T(8,128)}, u32[]{:S(2)}) copy-start(f32[2,2,384,128]{3,2,1,0:T(8,128)} %get-tuple-element.20) | copy-start | bytes 2359300
  90.1 12.0 %collective-permute-start.14 = (bf16[2,2,384,128]{3,2,1,0:T(8,128)(2,1)S(1)}, bf16[2,2,384,128]{3,2,1,0:T(8,128)(2,1)S(1)}, u32[]{:S(2)}, u32[]{:S(2)}) collective-permute-start(bf16[2,2,384,128]{3,2,1,0:T(8,128)(2,1)S(1)} %add_convert_fusion.1), channel_id=1, source_target_pairs={{2,0},{4,2},{6,4},{8,6},{10,8},{12,10},{14,12},{16,14},{18,16},{20... | collective-permute-start | bytes 1179656 | tf_op jit(solution)/shard_map/ppermute | solution.py:19
  101.9 1.1 %copy-start.2 = (bf16[192,32,128]{2,1,0:T(8,128)(2,1)}, bf16[192,32,128]{2,1,0:T(8,128)(2,1)S(1)}, u32[]{:S(2)}) copy-start(bf16[192,32,128]{2,1,0:T(8,128)(2,1)S(1)} %constant_dynamic-update-slice_fusion.2) | copy-start | bytes 4718596
